TPU v7x, 256 devices: a whole 4x4x8 slice. The times are simulated.
256 devices in a mesh: section: 16 (over x, y), tensor: 16 (over z, core).
Axes of the slice: x: 4, y: 4, z: 8, core: 2. Of those that a mesh axis runs over, the one named last changes fastest.
Arguments:
- queries: bfloat16 [16, 512, 8192], P('section', None, 'tensor'), may hold values from -20 to 20
- key_rows: bfloat16 [16, 512, 1024], P('section'), may hold values from -6 to 6
- value_rows: bfloat16 [16, 512, 1024], P('section'), may hold values from -6 to 6
- out_grad: bfloat16 [16, 512, 8192], P('section', None, 'tensor'), may hold values from -24 to 24
- layer_input: bfloat16 [16, 512, 8192], P('section', 'tensor'), may hold values from -64 to 64
- query_weight: bfloat16 [16, 8192, 8192], P('section', None, 'tensor'), may hold values from -0.0625 to 0.0625
- dion_basis: float32 [16, 8192, 256], P('section', 'tensor'), may hold values from -0.0625 to 0.0625
- lengths: int32 [16, 3], P('section'), may hold values from 1 to 256, 512 in all within a row
Outputs:
- upstream: bfloat16 [16, 512, 8192], P('section', 'tensor')
- left_factor: float32 [16, 8192, 256], P('section', 'tensor')
- right_factor: float32 [16, 8192, 256], P('section', 'tensor')
Inputs may be any that keep to these rules, and one draw needn't show every extreme that they name: For each section the lengths of the prompt, the chosen and the rejected response, in that order, summing to 512.
All inputs are finite; a program needn't handle non-finite values.
Results may differ from a plain program's by a relative error of at most 0.022.
Values may be sent and summed in bfloat16 or wider, within the bound.
No kernel may reach another device: no remote copies, remote signals or barrier semaphores. Data moves between devices by JAX's collectives and lax.ppermute only.
A program may use at most 64 MiB of HBM per device.

v0:
```python
import math
import jax
import jax.numpy as jnp
from jax import lax
from jax.sharding import PartitionSpec as P

D = 8192
HD = 128
GROUP = 8
rope_base = 500000.0
highest = lax.Precision.HIGHEST


def shifted(value, axis, steps):
    count = lax.axis_size(axis)
    first, last = (max(0, -steps), min(count, count - steps))
    return lax.ppermute(value, axis, [(source, source + steps) for source in range(first, last)])


def tree_layout(lengths_row, token_count):
    token_ids = jnp.arange(token_count, dtype=jnp.int32)
    bound_one = lengths_row[0]
    bound_two = lengths_row[0] + lengths_row[1]
    positions = jnp.where(token_ids < bound_two, token_ids, token_ids - lengths_row[1]).astype(
        jnp.float32
    )
    row_ids = token_ids[:, None]
    col_ids = token_ids[None, :]
    crossed = (row_ids >= bound_two) & (col_ids >= bound_one) & (col_ids < bound_two)
    visible = (col_ids <= row_ids) & jnp.logical_not(crossed)
    return (positions, visible)


def unrotate(rotated, positions):
    head_dim = rotated.shape[-1]
    half_dim = head_dim // 2
    freq_ids = jnp.arange(half_dim, dtype=jnp.float32)
    inverse = jnp.exp(-math.log(rope_base) * 2.0 * freq_ids / head_dim)
    angles = positions[:, None] * inverse[None, :]
    cosine = jnp.cos(angles)[:, None, :]
    sine_part = jnp.sin(angles)[:, None, :]
    first_half = rotated[..., :half_dim]
    second_half = rotated[..., half_dim:]
    return jnp.concatenate(
        [
            first_half * cosine + second_half * sine_part,
            second_half * cosine - first_half * sine_part,
        ],
        axis=-1,
    )


def local_backward(query_heads, grad_heads, key_block, value_block, visible):
    score_scale = 1.0 / math.sqrt(query_heads.shape[-1])
    scores = (
        jnp.einsum("qhd,kd->hqk", query_heads, key_block, preferred_element_type=jnp.float32)
        * score_scale
    )
    scores = jnp.where(visible[None], scores, -jnp.inf)
    row_max = jnp.max(scores, axis=-1, keepdims=True)
    exp_scores = jnp.exp(scores - row_max)
    weights = exp_scores / jnp.sum(exp_scores, axis=-1, keepdims=True)
    weights_low = weights.astype(jnp.bfloat16)
    outputs = jnp.einsum(
        "hqk,kd->qhd", weights_low, value_block, preferred_element_type=jnp.float32
    )
    out_dot = jnp.sum(grad_heads.astype(jnp.float32) * outputs, axis=-1)
    prob_grad = jnp.einsum(
        "qhd,kd->hqk", grad_heads, value_block, preferred_element_type=jnp.float32
    )
    score_grad = (weights * (prob_grad - out_dot.T[:, :, None])).astype(jnp.bfloat16)
    return (
        jnp.einsum("hqk,kd->qhd", score_grad, key_block, preferred_element_type=jnp.float32)
        * score_scale
    )


def local(queries, key_rows, value_rows, out_grad, layer_input, query_weight, dion_basis, lengths):
    token_count = queries.shape[1]
    local_width = queries.shape[2]
    local_heads = local_width // HD
    tensor_count = lax.axis_size("tensor")
    tensor_index = lax.axis_index("tensor")
    col_width = D // tensor_count
    gathered = lax.all_gather(layer_input[0], "tensor", axis=0, tiled=True)
    columns = lax.dynamic_slice_in_dim(gathered, tensor_index * col_width, col_width, 1)
    positions, visible = tree_layout(lengths[0], token_count)
    group_head = tensor_index * local_heads // GROUP
    key_block = lax.dynamic_slice_in_dim(key_rows[0], group_head * HD, HD, 1)
    value_block = lax.dynamic_slice_in_dim(value_rows[0], group_head * HD, HD, 1)
    rotated = local_backward(
        queries[0].reshape(token_count, local_heads, HD),
        out_grad[0].reshape(token_count, local_heads, HD),
        key_block,
        value_block,
        visible,
    )
    query_grad = unrotate(rotated, positions).reshape(token_count, local_width).astype(jnp.bfloat16)
    weight_local = query_weight[0]
    layer_grad = lax.psum_scatter(
        lax.dot_general(
            query_grad, weight_local, (((1,), (1,)), ((), ())), preferred_element_type=jnp.float32
        ).astype(jnp.bfloat16),
        "tensor",
        scatter_dimension=0,
        tiled=True,
    )
    upstream = shifted(layer_grad, "section", -1)
    grad_wide = query_grad.astype(jnp.float32)
    projected = lax.psum(jnp.dot(grad_wide, dion_basis[0], precision=highest), "tensor")
    column_wide = columns.astype(jnp.float32)
    left_raw = lax.dot_general(column_wide, projected, (((0,), (0,)), ((), ())), precision=highest)
    gram_part = lax.dot_general(left_raw, left_raw, (((0,), (0,)), ((), ())), precision=highest)
    mixed_part = jnp.dot(column_wide, left_raw, precision=highest)
    gram_total, mixed_total = lax.psum((gram_part, mixed_part), "tensor")
    lower_factor = jnp.linalg.cholesky(gram_total)
    left_orth = lax.linalg.triangular_solve(
        lower_factor, left_raw, left_side=False, lower=True, transpose_a=True
    )
    mixed_orth = lax.linalg.triangular_solve(
        lower_factor, mixed_total, left_side=False, lower=True, transpose_a=True
    )
    right_factor = lax.dot_general(
        grad_wide, mixed_orth, (((0,), (0,)), ((), ())), precision=highest
    )
    return (upstream[None], (left_orth * math.sqrt(D))[None], right_factor[None])


def solution(mesh):
    placed = (
        P("section", None, "tensor"),
        P("section", None, None),
        P("section", None, None),
        P("section", None, "tensor"),
        P("section", "tensor", None),
        P("section", None, "tensor"),
        P("section", "tensor", None),
        P("section", None),
    )
    return jax.shard_map(
        local,
        mesh=mesh,
        in_specs=placed,
        out_specs=(
            P("section", "tensor", None),
            P("section", "tensor", None),
            P("section", "tensor", None),
        ),
        check_vma=False,
    )
```

profile of v0, /device:TPU:26, one launch (start us, length us, event | category | flops | bytes accessed | tf_op | source)
XLA Modules:
  0.0 409.4 jit_solution(8106175779800506039)
XLA Ops:
  7.2 1.3 fusion.63
  8.6 0.6 iota_compare_fusion.5
  10.5 0.7 select_convert_fusion
  11.2 1.2 reshape_squeeze.6
  12.4 0.7 fusion.27
  13.4 2.1 fusion.64
  15.5 1.9 copy-done.3
  17.4 1.4 fusion.5
  18.8 0.4 copy.25
  19.2 1.2 reshape_squeeze.7
  20.4 0.6 fusion.13
  21.1 3.5 fusion.12
  24.6 0.5 multiply_cosine_fusion
  25.4 1.5 fusion.19
  27.0 0.7 all-gather.3.cloned.1.call-update
  27.7 111.7 %all-reduce.5.cloned.1.call-done = f32[512,256]{1,0:T(8,128)} async-done(((f32[512,256]{1,0:T(8,128)}), f32[512,256]{1,0:T(8,128)}) %all-reduce.5.cloned.1.call-update) | async-done | bytes 524304 | tf_op jit(solution)/shard_map/psum | solution.py:110
  139.4 58.2 %all-gather.3.cloned.1.call-done = bf16[1,512,8192]{2,1,0:T(8,128)(2,1)} async-done(((bf16[1,32,8192]{2,1,0:T(8,128)(2,1)}), bf16[1,512,8192]{2,1,0:T(8,128)(2,1)}) %all-gather.3.cloned.1.call-update) | async-done | bytes 8388624 | tf_op jit(solution)/shard_map/all_gather | solution.py:85
  197.7 1.9 fusion.23
  199.6 1.7 fusion.65
  201.3 2.5 fusion.21
  203.9 10.2 %convolution_convert_fusion = bf16[512,8192]{1,0:T(8,128)(2,1)} fusion(bf16[512,512]{0,1:T(8,128)(2,1)S(1)} %bitcast.114, bf16[1,8192,512]{2,1,0:T(8,128)(2,1)} %param.15), kind=kOutput, calls=%fused_computation.3 | convolution fusion | flops 4299161600 | bytes 17301504 | tf_op jit(solution)/shard_map/dot_general | solution.py:101
  214.1 99.1 %all-reduce.7.cloned.1.call-done = (f32[256,256]{0,1:T(8,128)}, f32[512,256]{1,0:T(8,128)}) async-done(((f32[256,256]{0,1:T(8,128)}, f32[512,256]{1,0:T(8,128)}), (f32[256,256]{0,1:T(8,128)}, f32[512,256]{1,0:T(8,128)})) %all-reduce.7.cloned.1.call-update) | async-done | bytes 786448 | tf_op jit(solution)/shard_map/psum | solution.py:115
  313.3 1.1 copy.22
  314.4 1.0 fusion.35
  315.4 11.7 %cholesky.50 = f32[128,128]{1,0:T(8,128)S(1)} custom-call(f32[128,128]{1,0:T(8,128)S(1)} %cholesky.118), custom_call_target="Cholesky" | custom-call | tf_op jit(solution)/shard_map/jit(cholesky)/cholesky | solution.py:116
  327.2 9.8 %custom-call.14 = f32[1,128,128]{1,2,0:T(8,128)S(1)} custom-call(f32[1,128,128]{2,1,0:T(8,128)S(1)} %get-tuple-element.43), custom_call_target="InvertDiagBlocksLowerTriangular" | custom-call | tf_op jit(solution)/shard_map/jit(cholesky)/cholesky | solution.py:116
  337.2 0.3 convolution_subtract_fusion.2
  337.5 11.7 %cholesky.105 = f32[128,128]{1,0:T(8,128)S(1)} custom-call(f32[128,128]{1,0:T(8,128)S(1)} %convolution_subtract_fusion.2), custom_call_target="Cholesky" | custom-call | tf_op jit(solution)/shard_map/jit(cholesky)/cholesky | solution.py:116
  349.2 0.6 compare_reduce_fusion
  349.9 0.6 compare_reduce_fusion.1
  351.9 4.0 while.4
  351.9 0.6 fusion.80
  352.5 1.4 bitcast_dynamic-update-slice_fusion.2
  353.9 0.6 fusion.80
  354.5 1.4 bitcast_dynamic-update-slice_fusion.2
  355.9 19.9 %custom-call.16 = f32[2,128,128]{1,2,0:T(8,128)S(1)} custom-call(f32[2,128,128]{2,1,0:T(8,128)S(1)} %get-tuple-element.18), custom_call_target="InvertDiagBlocksLowerTriangular" | custom-call | tf_op jit(solution)/shard_map/triangular_solve/custom-call.0 | solution.py:117
  375.8 0.4 fusion.33
  376.2 0.6 convolution_subtract_fusion.1
  376.8 0.4 fusion.50
  377.3 1.0 copy.23
  378.3 0.4 fusion.31
  378.8 8.2 %reduce-scatter.2.cloned.1.call-done = bf16[32,8192]{1,0:T(8,128)(2,1)} async-done(((bf16[512,8192]{1,0:T(8,128)(2,1)}), bf16[32,8192]{1,0:T(8,128)(2,1)}) %reduce-scatter.2.cloned.1.call-update) | async-done | bytes 524304 | tf_op jit(solution)/shard_map/reduce_scatter | solution.py:100
  387.0 2.8 collective-permute-start
  389.8 0.6 convolution_subtract_fusion
  390.4 0.4 fusion.49
  390.8 1.4 convolution_bitcast_fusion
  392.2 9.8 %collective-permute-done = bf16[32,8192]{1,0:T(8,128)(2,1)S(1)} collective-permute-done((bf16[32,8192]{1,0:T(8,128)(2,1)}, bf16[32,8192]{1,0:T(8,128)(2,1)S(1)}, u32[]{:S(2)}, u32[]{:S(2)}) %collective-permute-start) | collective-permute-done | bytes 524320 | tf_op jit(solution)/shard_map/ppermute | solution.py:17
  402.1 0.8 copy.50
  (32 shorter events, 1.3 us)
Async XLA Ops:
  7.2 5.2 %copy-start = (bf16[1,512,1024]{2,1,0:T(8,128)(2,1)S(1)}, bf16[1,512,1024]{2,1,0:T(8,128)(2,1)}, u32[]{:S(2)}) copy-start(bf16[1,512,1024]{2,1,0:T(8,128)(2,1)} %param.11) | copy-start | bytes 3145732
  7.2 132.2 %all-reduce.5.cloned.1.call-start = ((), (), s32[]{:S(2)}) async-start(), calls=%async_computation.2 | async-start | bytes 1048576 | tf_op jit(solution)/shard_map/psum | solution.py:110
  15.5 1.9 copy-start.3
  21.1 4.2 %copy-start.1 = (f32[1,512,256]{2,1,0:T(8,128)S(1)}, f32[1,512,256]{2,1,0:T(8,128)}, u32[]{:S(2)}) copy-start(f32[1,512,256]{2,1,0:T(8,128)} %param.16) | copy-start | bytes 1572868
  26.9 170.7 %all-gather.3.cloned.1.call-start = ((), (), s32[]{:S(2)}) async-start(), calls=%async_computation.3 | async-start | bytes 8912896 | tf_op jit(solution)/shard_map/all_gather | solution.py:85
  27.7 285.6 %all-reduce.7.cloned.1.call-start = ((), (), s32[]{:S(2)}) async-start(), calls=%async_computation.4 | async-start | bytes 1572864 | tf_op jit(solution)/shard_map/psum | solution.py:115
  203.8 183.2 %reduce-scatter.2.cloned.1.call-start = ((), (), s32[]{:S(2)}) async-start(), calls=%async_computation.1 | async-start | bytes 8912896 | tf_op jit(solution)/shard_map/reduce_scatter | solution.py:100
  313.3 65.1 %copy-start.2 = (f32[512,256]{1,0:T(8,128)S(1)}, f32[512,256]{1,0:T(8,128)}, u32[]{:S(2)}) copy-start(f32[512,256]{1,0:T(8,128)} %get-tuple-element.35) | copy-start | bytes 1572868
  387.0 15.1 %collective-permute-start = (bf16[32,8192]{1,0:T(8,128)(2,1)}, bf16[32,8192]{1,0:T(8,128)(2,1)S(1)}, u32[]{:S(2)}, u32[]{:S(2)}) collective-permute-start(bf16[32,8192]{1,0:T(8,128)(2,1)} %reduce-scatter.2.cloned.1.call-done), channel_id=1, source_target_pairs={{16,0},{32,16},{48,32},{64,48},{80,64},{96,80},{112,96},{128,112},... | collective-permute-start | bytes 1572872 | tf_op jit(solution)/shard_map/ppermute | solution.py:17
Sparse Core Ops, SparseCore 0:
  27.1 112.3 all-reduce.4
  141.4 56.2 all-gather.2
  203.9 109.2 all-reduce.6
  315.7 71.2 reduce-scatter.1
where the time goes:
time: 410 us; the launch traced here: 409 us
  waiting for transfers between devices  288 us (70%)
  other arithmetic  60.6 us (15%)
  matrix products  28.2 us (7%)
  between operations  16.7 us (4%)
  local copies, waits for them, and re-layouts  13.1 us (3%)
    psum x1, waiting for transfers between devices, local(): lax.psum(jnp.dot(grad_wide, dion_basis[0], precision=highest), 'tensor')  112 us
    psum x1, waiting for transfers between devices, local(): gram_total, mixed_total = lax.psum((gram_part, mixed_part), 'tensor')  99.1 us
    all_gather x1, waiting for transfers between devices, local(): gathered = lax.all_gather(layer_input[0], 'tensor', axis=0, tiled=True)  58.2 us
    another operation x7, other arithmetic, local(): lower_factor = jnp.linalg.cholesky(gram_total)  34.6 us
    another operation x4, other arithmetic, local(): lax.linalg.triangular_solve(lower_factor, left_raw, left_side=False, lowe...  19.9 us
    dot_general x1, matrix products, local(): lax.dot_general(query_grad, weight_local, (((1,), (1,)), ((), ())), prefe...  10.2 us
    ppermute x1, waiting for transfers between devices, shifted(): lax.ppermute(value, axis, [(source, source + steps) for source in range(f...  9.81 us
    reduce_scatter x1, waiting for transfers between devices, local(): lax.psum_scatter(lax.dot_general(query_grad, weight_local, (((1,), (1,)),...  8.25 us
  transfers between devices with their start and end apart: 5, of which 5 were waited for; matrix products, arithmetic and copies ran while one was open for 19% of the time, Pallas kernels for 0%

commit v1 on v0

--- a/solution.py
+++ b/solution.py
@@ -1,14 +1,52 @@
+import functools
 import math
 import jax
 import jax.numpy as jnp
 from jax import lax
 from jax.sharding import PartitionSpec as P
+from jax.lax import axis_index, axis_size, ppermute
 
 D = 8192
 HD = 128
 GROUP = 8
 rope_base = 500000.0
 highest = lax.Precision.HIGHEST
+
+
+def drive_groups_by_axis(block_here, axis_tag):
+    t_next, w_next, front = (axis_size(axis_tag), axis_index(axis_tag), block_here.shape[0])
+    it = 0
+    pages = []
+    while it < t_next:
+        pages.append((it, (it + 1) % t_next))
+        it = it + 1
+    it = 0
+    line_up = []
+    while it < t_next:
+        line_up.append((it, (it - 1) % t_next))
+        it = it + 1
+    n_now = jnp.zeros(
+        (*block_here.shape[:0], t_next * front, *block_here.shape[1:]), block_here.dtype
+    )
+    n_now = lax.dynamic_update_slice_in_dim(n_now, block_here, w_next * front, axis=0)
+    met_up = val = block_here
+    answer = t_next // 2
+    b = 1
+    while b < answer + 1:
+        met_up = ppermute(met_up, axis_tag, pages)
+        n_now = lax.dynamic_update_slice_in_dim(
+            n_now, met_up, (w_next - b) % t_next * front, axis=0
+        )
+        if b < t_next - answer:
+            val = ppermute(val, axis_tag, line_up)
+            n_now = lax.dynamic_update_slice_in_dim(
+                n_now, val, (w_next + b) % t_next * front, axis=0
+            )
+        b = b + 1
+    return n_now
+
+
+hold_kinds_on_mesh = functools.partial(drive_groups_by_axis, axis_tag="tensor")
 
 
 def shifted(value, axis, steps):
@@ -82,7 +120,7 @@
     tensor_count = lax.axis_size("tensor")
     tensor_index = lax.axis_index("tensor")
     col_width = D // tensor_count
-    gathered = lax.all_gather(layer_input[0], "tensor", axis=0, tiled=True)
+    gathered = hold_kinds_on_mesh(layer_input[0])
     columns = lax.dynamic_slice_in_dim(gathered, tensor_index * col_width, col_width, 1)
     positions, visible = tree_layout(lengths[0], token_count)
     group_head = tensor_index * local_heads // GROUP

time: 410 us -> 358 us (0.87)
  waiting for transfers between devices: 288 us -> 190 us
  starting transfers between devices: 2.95 us -> 26.1 us
  local copies, waits for them, and re-layouts: 13.1 us -> 33.4 us
    psum x1, waiting for transfers between devices: 112 us -> 34 us  [local(): lax.psum(jnp.dot(grad_wide, dion_basis[0], precision=highest), 'tensor')]
    all_gather x1 -> x0, waiting for transfers between devices: 58.2 us -> none  [local(): gathered = lax.all_gather(layer_input[0], 'tensor', axis=0, tiled=True)]
    ppermute x0 -> x15, waiting for transfers between devices: none -> 39.4 us  [the longest x8 39.4 us: drive_groups_by_axis(): met_up = ppermute(met_up, axis_tag, pages)]
    ppermute x0 -> x15, starting transfers between devices: none -> 23.1 us  [the longest x7 23 us: drive_groups_by_axis(): val = ppermute(val, axis_tag, line_up)]
    dynamic_update_slice x0 -> x16, local copies, waits for them, and re-layouts: none -> 15.5 us  [the longest x8 7.73 us: drive_groups_by_axis(): lax.dynamic_update_slice_in_dim(n_now, met_up, (w_next - b) % t_next * fr...]
    broadcast_in_dim x0 -> x1, local copies, waits for them, and re-layouts: none -> 4.24 us  [drive_groups_by_axis(): jnp.zeros((*block_here.shape[:0], t_next * front, *block_here.shape[1:]),...]
  transfers between devices with their start and end apart: 5 -> 19, of which waited for: 5 -> 11; matrix products, arithmetic and copies ran while one was open for 19% -> 32% of each run, Pallas kernels for 0% -> 0%
where the time goes in v1:
time: 358 us; the launch traced here: 357 us
  waiting for transfers between devices  190 us (53%)
  other arithmetic  61.2 us (17%)
  local copies, waits for them, and re-layouts  33.4 us (9%)
  matrix products  29.2 us (8%)
  starting transfers between devices  26.1 us (7%)
  between operations  16.7 us (5%)
    psum x1, waiting for transfers between devices, local(): gram_total, mixed_total = lax.psum((gram_part, mixed_part), 'tensor')  101 us
    ppermute x8, waiting for transfers between devices, drive_groups_by_axis(): met_up = ppermute(met_up, axis_tag, pages)  39.4 us
    another operation x7, other arithmetic, local(): lower_factor = jnp.linalg.cholesky(gram_total)  34.6 us
    psum x1, waiting for transfers between devices, local(): lax.psum(jnp.dot(grad_wide, dion_basis[0], precision=highest), 'tensor')  34 us
    ppermute x7, starting transfers between devices, drive_groups_by_axis(): val = ppermute(val, axis_tag, line_up)  23 us
    another operation x4, other arithmetic, local(): lax.linalg.triangular_solve(lower_factor, left_raw, left_side=False, lowe...  20.5 us
    dot_general x1, matrix products, local(): lax.dot_general(query_grad, weight_local, (((1,), (1,)), ((), ())), prefe...  10.2 us
    ppermute x1, waiting for transfers between devices, shifted(): lax.ppermute(value, axis, [(source, source + steps) for source in range(f...  9.87 us
  transfers between devices with their start and end apart: 19, of which 11 were waited for; matrix products, arithmetic and copies ran while one was open for 32% of the time, Pallas kernels for 0%

profile of v1, /device:TPU:26, one launch (start us, length us, event | category | flops | bytes accessed | tf_op | source)
XLA Modules:
  0.0 357.0 jit_solution(9803714601794097048)
XLA Ops:
  7.3 5.3 %collective-permute-start.2 = (bf16[32,8192]{1,0:T(8,128)(2,1)}, bf16[32,8192]{1,0:T(8,128)(2,1)}, u32[]{:S(2)}, u32[]{:S(2)}) collective-permute-start(bf16[32,8192]{1,0:T(8,128)(2,1)} %bitcast.116), channel_id=1, source_target_pairs={{0,15},{1,0},{2,1},{3,2},{4,3},{5,4},{6,5},{7,6},{8,7},{9,8},{10,9... | collective-permute-start | bytes 1572872 | tf_op jit(solution)/shard_map/ppermute | solution.py:41
  12.6 1.3 fusion.63
  16.5 1.2 reshape_squeeze.6
  18.7 2.1 fusion.64
  20.8 1.9 copy-done.5
  22.8 1.4 fusion.5
  24.6 1.2 reshape_squeeze.7
  26.5 3.5 fusion.12
  30.7 1.5 fusion.19
  32.3 4.2 %broadcast_in_dim.39 = bf16[512,8192]{1,0:T(8,128)(2,1)} broadcast(bf16[]{:T(256)} %constant.196.clone.1), dimensions={} | broadcast | bytes 8388610 | tf_op jit(solution)/shard_map/broadcast_in_dim | solution.py:28
  37.4 3.0 collective-permute-start.4
  40.4 1.9 constant_dynamic-update-slice_fusion.15
  42.3 1.9 constant_dynamic-update-slice_fusion.14
  44.1 3.5 collective-permute-done.3
  47.6 3.0 collective-permute-start.6
  51.4 0.9 constant_dynamic-update-slice_fusion.12
  52.3 5.5 %collective-permute-done.5 = bf16[32,8192]{1,0:T(8,128)(2,1)S(1)} collective-permute-done((bf16[32,8192]{1,0:T(8,128)(2,1)S(1)}, bf16[32,8192]{1,0:T(8,128)(2,1)S(1)}, u32[]{:S(2)}, u32[]{:S(2)}) %collective-permute-start.5) | collective-permute-done | bytes 524320 | tf_op jit(solution)/shard_map/ppermute | solution.py:36
  57.8 3.0 collective-permute-start.8
  62.4 5.6 %collective-permute-done.7 = bf16[32,8192]{1,0:T(8,128)(2,1)S(1)} collective-permute-done((bf16[32,8192]{1,0:T(8,128)(2,1)S(1)}, bf16[32,8192]{1,0:T(8,128)(2,1)S(1)}, u32[]{:S(2)}, u32[]{:S(2)}) %collective-permute-start.7) | collective-permute-done | bytes 524320 | tf_op jit(solution)/shard_map/ppermute | solution.py:36
  68.0 3.0 collective-permute-start.10
  72.6 5.5 %collective-permute-done.9 = bf16[32,8192]{1,0:T(8,128)(2,1)S(1)} collective-permute-done((bf16[32,8192]{1,0:T(8,128)(2,1)S(1)}, bf16[32,8192]{1,0:T(8,128)(2,1)S(1)}, u32[]{:S(2)}, u32[]{:S(2)}) %collective-permute-start.9) | collective-permute-done | bytes 524320 | tf_op jit(solution)/shard_map/ppermute | solution.py:36
  78.1 3.0 collective-permute-start.12
  82.8 5.6 %collective-permute-done.11 = bf16[32,8192]{1,0:T(8,128)(2,1)S(1)} collective-permute-done((bf16[32,8192]{1,0:T(8,128)(2,1)S(1)}, bf16[32,8192]{1,0:T(8,128)(2,1)S(1)}, u32[]{:S(2)}, u32[]{:S(2)}) %collective-permute-start.11) | collective-permute-done | bytes 524320 | tf_op jit(solution)/shard_map/ppermute | solution.py:36
  88.3 3.0 collective-permute-start.14
  91.3 0.9 constant_dynamic-update-slice_fusion.5
  93.0 5.1 %collective-permute-done.13 = bf16[32,8192]{1,0:T(8,128)(2,1)S(1)} collective-permute-done((bf16[32,8192]{1,0:T(8,128)(2,1)S(1)}, bf16[32,8192]{1,0:T(8,128)(2,1)S(1)}, u32[]{:S(2)}, u32[]{:S(2)}) %collective-permute-start.13) | collective-permute-done | bytes 524320 | tf_op jit(solution)/shard_map/ppermute | solution.py:36
  99.8 8.6 %collective-permute-done.15 = bf16[32,8192]{1,0:T(8,128)(2,1)S(1)} collective-permute-done((bf16[32,8192]{1,0:T(8,128)(2,1)S(1)}, bf16[32,8192]{1,0:T(8,128)(2,1)S(1)}, u32[]{:S(2)}, u32[]{:S(2)}) %collective-permute-start.15) | collective-permute-done | bytes 524320 | tf_op jit(solution)/shard_map/ppermute | solution.py:36
  109.2 34.0 %all-reduce.5.cloned.1.call-done = f32[512,256]{1,0:T(8,128)} async-done(((f32[512,256]{1,0:T(8,128)}), f32[512,256]{1,0:T(8,128)}) %all-reduce.5.cloned.1.call-update) | async-done | bytes 524304 | tf_op jit(solution)/shard_map/psum | solution.py:148
  143.2 1.9 fusion.27
  145.2 2.5 fusion.25
  147.7 1.7 fusion.65
  149.6 10.2 %convolution_convert_fusion = bf16[512,8192]{1,0:T(8,128)(2,1)} fusion(bf16[512,512]{0,1:T(8,128)(2,1)S(1)} %bitcast.109, bf16[1,8192,512]{2,1,0:T(8,128)(2,1)} %param.15), kind=kOutput, calls=%fused_computation.3 | convolution fusion | flops 4299161600 | bytes 17301504 | tf_op jit(solution)/shard_map/dot_general | solution.py:139
  159.9 100.9 %all-reduce.7.cloned.1.call-done = (f32[256,256]{0,1:T(8,128)}, f32[512,256]{1,0:T(8,128)}) async-done(((f32[256,256]{0,1:T(8,128)}, f32[512,256]{1,0:T(8,128)}), (f32[256,256]{0,1:T(8,128)}, f32[512,256]{1,0:T(8,128)})) %all-reduce.7.cloned.1.call-update) | async-done | bytes 786448 | tf_op jit(solution)/shard_map/psum | solution.py:153
  260.8 1.1 copy.22
  262.0 1.0 fusion.35
  263.0 11.7 %cholesky.50 = f32[128,128]{1,0:T(8,128)S(1)} custom-call(f32[128,128]{1,0:T(8,128)S(1)} %cholesky.118), custom_call_target="Cholesky" | custom-call | tf_op jit(solution)/shard_map/jit(cholesky)/cholesky | solution.py:154
  274.7 9.8 %custom-call.14 = f32[1,128,128]{1,2,0:T(8,128)S(1)} custom-call(f32[1,128,128]{2,1,0:T(8,128)S(1)} %get-tuple-element.43), custom_call_target="InvertDiagBlocksLowerTriangular" | custom-call | tf_op jit(solution)/shard_map/jit(cholesky)/cholesky | solution.py:154
  285.0 11.7 %cholesky.105 = f32[128,128]{1,0:T(8,128)S(1)} custom-call(f32[128,128]{1,0:T(8,128)S(1)} %convolution_subtract_fusion), custom_call_target="Cholesky" | custom-call | tf_op jit(solution)/shard_map/jit(cholesky)/cholesky | solution.py:154
  299.5 4.0 %while.4 = (s32[]{:T(128)}, f32[256,256]{1,0:T(8,128)S(1)}, s32[2,2]{1,0:T(2,128)S(1)}, f32[2,128,128]{2,1,0:T(8,128)S(1)}, s32[]{:T(128)}) while((s32[]{:T(128)}, f32[256,256]{1,0:T(8,128)S(1)}, s32[2,2]{1,0:T(2,128)S(1)}, f32[2,128,128]{2,1,0:T(8,128)S(1)}, s32[]{:T(128)}) %tuple.38), condition=%wide.while_cond, body=%wide.while_body.sunk | while | flops 2 | bytes 131181 | solution.py:155
  300.1 1.4 bitcast_dynamic-update-slice_fusion.2
  302.1 1.4 bitcast_dynamic-update-slice_fusion.2
  304.1 20.5 %custom-call.16 = f32[2,128,128]{1,2,0:T(8,128)S(1)} custom-call(f32[2,128,128]{2,1,0:T(8,128)} %copy-done.4), custom_call_target="InvertDiagBlocksLowerTriangular" | custom-call | tf_op jit(solution)/shard_map/triangular_solve/custom-call.0 | solution.py:155
  326.1 1.0 copy.23
  327.1 1.4 fusion.30
  328.5 6.0 %reduce-scatter.2.cloned.1.call-done = bf16[32,8192]{1,0:T(8,128)(2,1)} async-done(((bf16[512,8192]{1,0:T(8,128)(2,1)}), bf16[32,8192]{1,0:T(8,128)(2,1)}) %reduce-scatter.2.cloned.1.call-update) | async-done | bytes 524304 | tf_op jit(solution)/shard_map/reduce_scatter | solution.py:138
  334.6 2.7 collective-permute-start
  338.3 1.4 convolution_bitcast_fusion
  339.8 9.9 %collective-permute-done = bf16[32,8192]{1,0:T(8,128)(2,1)S(1)} collective-permute-done((bf16[32,8192]{1,0:T(8,128)(2,1)}, bf16[32,8192]{1,0:T(8,128)(2,1)S(1)}, u32[]{:S(2)}, u32[]{:S(2)}) %collective-permute-start) | collective-permute-done | bytes 524320 | tf_op jit(solution)/shard_map/ppermute | solution.py:55
  (80 shorter events, 21.6 us)
Async XLA Ops:
  7.2 10.5 %copy-start = (bf16[1,512,1024]{2,1,0:T(8,128)(2,1)S(1)}, bf16[1,512,1024]{2,1,0:T(8,128)(2,1)}, u32[]{:S(2)}) copy-start(bf16[1,512,1024]{2,1,0:T(8,128)(2,1)} %param.11) | copy-start | bytes 3145732
  7.2 136.1 %all-reduce.5.cloned.1.call-start = ((), (), s32[]{:S(2)}) async-start(), calls=%async_computation.2 | async-start | bytes 1048576 | tf_op jit(solution)/shard_map/psum | solution.py:148
  7.2 30.2 %collective-permute-start.1 = (bf16[32,8192]{1,0:T(8,128)(2,1)}, bf16[32,8192]{1,0:T(8,128)(2,1)}, u32[]{:S(2)}, u32[]{:S(2)}) collective-permute-start(bf16[32,8192]{1,0:T(8,128)(2,1)} %bitcast.115), channel_id=1, source_target_pairs={{0,1},{1,2},{2,3},{3,4},{4,5},{5,6},{6,7},{7,8},{8,9},{9,10},{10,1... | collective-permute-start | bytes 1572872 | tf_op jit(solution)/shard_map/ppermute | solution.py:36
  7.3 30.2 %collective-permute-start.2 = (bf16[32,8192]{1,0:T(8,128)(2,1)}, bf16[32,8192]{1,0:T(8,128)(2,1)}, u32[]{:S(2)}, u32[]{:S(2)}) collective-permute-start(bf16[32,8192]{1,0:T(8,128)(2,1)} %bitcast.116), channel_id=1, source_target_pairs={{0,15},{1,0},{2,1},{3,2},{4,3},{5,4},{6,5},{7,6},{8,7},{9,8},{10,9... | collective-permute-start | bytes 1572872 | tf_op jit(solution)/shard_map/ppermute | solution.py:41
  20.8 1.9 copy-start.5
  26.5 4.3 %copy-start.1 = (f32[1,512,256]{2,1,0:T(8,128)S(1)}, f32[1,512,256]{2,1,0:T(8,128)}, u32[]{:S(2)}) copy-start(f32[1,512,256]{2,1,0:T(8,128)} %param.16) | copy-start | bytes 1572868
  29.9 6.6 %copy-start.3 = (bf16[1,32,8192]{2,1,0:T(8,128)(2,1)S(1)}, bf16[1,32,8192]{2,1,0:T(8,128)(2,1)}, u32[]{:S(2)}) copy-start(bf16[1,32,8192]{2,1,0:T(8,128)(2,1)} %param.14) | copy-start | bytes 1572868
  32.3 228.5 %all-reduce.7.cloned.1.call-start = ((), (), s32[]{:S(2)}) async-start(), calls=%async_computation.3 | async-start | bytes 1572864 | tf_op jit(solution)/shard_map/psum | solution.py:153
  37.4 10.2 %collective-permute-start.3 = (bf16[32,8192]{1,0:T(8,128)(2,1)}, bf16[32,8192]{1,0:T(8,128)(2,1)S(1)}, u32[]{:S(2)}, u32[]{:S(2)}) collective-permute-start(bf16[32,8192]{1,0:T(8,128)(2,1)} %collective-permute-done.1), channel_id=1, source_target_pairs={{0,1},{1,2},{2,3},{3,4},{4,5},{5,6},{6,7},{7,8},{8,9},{9,10},{10,1... | collective-permute-start | bytes 1572872 | tf_op jit(solution)/shard_map/ppermute | solution.py:36
  37.4 10.2 %collective-permute-start.4 = (bf16[32,8192]{1,0:T(8,128)(2,1)}, bf16[32,8192]{1,0:T(8,128)(2,1)S(1)}, u32[]{:S(2)}, u32[]{:S(2)}) collective-permute-start(bf16[32,8192]{1,0:T(8,128)(2,1)} %collective-permute-done.2), channel_id=1, source_target_pairs={{0,15},{1,0},{2,1},{3,2},{4,3},{5,4},{6,5},{7,6},{8,7},{9,8},{10,9... | collective-permute-start | bytes 1572872 | tf_op jit(solution)/shard_map/ppermute | solution.py:41
  47.6 10.2 %collective-permute-start.5 = (bf16[32,8192]{1,0:T(8,128)(2,1)S(1)}, bf16[32,8192]{1,0:T(8,128)(2,1)S(1)}, u32[]{:S(2)}, u32[]{:S(2)}) collective-permute-start(bf16[32,8192]{1,0:T(8,128)(2,1)S(1)} %collective-permute-done.3), channel_id=1, source_target_pairs={{0,1},{1,2},{2,3},{3,4},{4,5},{5,6},{6,7},{7,8},{8,9},{9,10},{10,1... | collective-permute-start | bytes 1572872 | tf_op jit(solution)/shard_map/ppermute | solution.py:36
  47.6 10.2 %collective-permute-start.6 = (bf16[32,8192]{1,0:T(8,128)(2,1)S(1)}, bf16[32,8192]{1,0:T(8,128)(2,1)S(1)}, u32[]{:S(2)}, u32[]{:S(2)}) collective-permute-start(bf16[32,8192]{1,0:T(8,128)(2,1)S(1)} %collective-permute-done.4), channel_id=1, source_target_pairs={{0,15},{1,0},{2,1},{3,2},{4,3},{5,4},{6,5},{7,6},{8,7},{9,8},{10,9... | collective-permute-start | bytes 1572872 | tf_op jit(solution)/shard_map/ppermute | solution.py:41
  57.8 10.2 %collective-permute-start.7 = (bf16[32,8192]{1,0:T(8,128)(2,1)S(1)}, bf16[32,8192]{1,0:T(8,128)(2,1)S(1)}, u32[]{:S(2)}, u32[]{:S(2)}) collective-permute-start(bf16[32,8192]{1,0:T(8,128)(2,1)S(1)} %collective-permute-done.5), channel_id=1, source_target_pairs={{0,1},{1,2},{2,3},{3,4},{4,5},{5,6},{6,7},{7,8},{8,9},{9,10},{10,1... | collective-permute-start | bytes 1572872 | tf_op jit(solution)/shard_map/ppermute | solution.py:36
  57.8 10.2 %collective-permute-start.8 = (bf16[32,8192]{1,0:T(8,128)(2,1)S(1)}, bf16[32,8192]{1,0:T(8,128)(2,1)S(1)}, u32[]{:S(2)}, u32[]{:S(2)}) collective-permute-start(bf16[32,8192]{1,0:T(8,128)(2,1)S(1)} %collective-permute-done.6), channel_id=1, source_target_pairs={{0,15},{1,0},{2,1},{3,2},{4,3},{5,4},{6,5},{7,6},{8,7},{9,8},{10,9... | collective-permute-start | bytes 1572872 | tf_op jit(solution)/shard_map/ppermute | solution.py:41
  68.0 10.2 %collective-permute-start.9 = (bf16[32,8192]{1,0:T(8,128)(2,1)S(1)}, bf16[32,8192]{1,0:T(8,128)(2,1)S(1)}, u32[]{:S(2)}, u32[]{:S(2)}) collective-permute-start(bf16[32,8192]{1,0:T(8,128)(2,1)S(1)} %collective-permute-done.7), channel_id=1, source_target_pairs={{0,1},{1,2},{2,3},{3,4},{4,5},{5,6},{6,7},{7,8},{8,9},{9,10},{10,1... | collective-permute-start | bytes 1572872 | tf_op jit(solution)/shard_map/ppermute | solution.py:36
  68.0 10.2 %collective-permute-start.10 = (bf16[32,8192]{1,0:T(8,128)(2,1)S(1)}, bf16[32,8192]{1,0:T(8,128)(2,1)S(1)}, u32[]{:S(2)}, u32[]{:S(2)}) collective-permute-start(bf16[32,8192]{1,0:T(8,128)(2,1)S(1)} %collective-permute-done.8), channel_id=1, source_target_pairs={{0,15},{1,0},{2,1},{3,2},{4,3},{5,4},{6,5},{7,6},{8,7},{9,8},{10,9... | collective-permute-start | bytes 1572872 | tf_op jit(solution)/shard_map/ppermute | solution.py:41
  78.1 10.2 %collective-permute-start.11 = (bf16[32,8192]{1,0:T(8,128)(2,1)S(1)}, bf16[32,8192]{1,0:T(8,128)(2,1)S(1)}, u32[]{:S(2)}, u32[]{:S(2)}) collective-permute-start(bf16[32,8192]{1,0:T(8,128)(2,1)S(1)} %collective-permute-done.9), channel_id=1, source_target_pairs={{0,1},{1,2},{2,3},{3,4},{4,5},{5,6},{6,7},{7,8},{8,9},{9,10},{10,1... | collective-permute-start | bytes 1572872 | tf_op jit(solution)/shard_map/ppermute | solution.py:36
  78.1 10.2 %collective-permute-start.12 = (bf16[32,8192]{1,0:T(8,128)(2,1)S(1)}, bf16[32,8192]{1,0:T(8,128)(2,1)S(1)}, u32[]{:S(2)}, u32[]{:S(2)}) collective-permute-start(bf16[32,8192]{1,0:T(8,128)(2,1)S(1)} %collective-permute-done.10), channel_id=1, source_target_pairs={{0,15},{1,0},{2,1},{3,2},{4,3},{5,4},{6,5},{7,6},{8,7},{9,8},{10,9... | collective-permute-start | bytes 1572872 | tf_op jit(solution)/shard_map/ppermute | solution.py:41
  88.3 9.8 %collective-permute-start.13 = (bf16[32,8192]{1,0:T(8,128)(2,1)S(1)}, bf16[32,8192]{1,0:T(8,128)(2,1)S(1)}, u32[]{:S(2)}, u32[]{:S(2)}) collective-permute-start(bf16[32,8192]{1,0:T(8,128)(2,1)S(1)} %collective-permute-done.11), channel_id=1, source_target_pairs={{0,1},{1,2},{2,3},{3,4},{4,5},{5,6},{6,7},{7,8},{8,9},{9,10},{10,1... | collective-permute-start | bytes 1572872 | tf_op jit(solution)/shard_map/ppermute | solution.py:36
  88.3 10.6 %collective-permute-start.14 = (bf16[32,8192]{1,0:T(8,128)(2,1)S(1)}, bf16[32,8192]{1,0:T(8,128)(2,1)S(1)}, u32[]{:S(2)}, u32[]{:S(2)}) collective-permute-start(bf16[32,8192]{1,0:T(8,128)(2,1)S(1)} %collective-permute-done.12), channel_id=1, source_target_pairs={{0,15},{1,0},{2,1},{3,2},{4,3},{5,4},{6,5},{7,6},{8,7},{9,8},{10,9... | collective-permute-start | bytes 1572872 | tf_op jit(solution)/shard_map/ppermute | solution.py:41
  98.1 10.2 %collective-permute-start.15 = (bf16[32,8192]{1,0:T(8,128)(2,1)S(1)}, bf16[32,8192]{1,0:T(8,128)(2,1)S(1)}, u32[]{:S(2)}, u32[]{:S(2)}) collective-permute-start(bf16[32,8192]{1,0:T(8,128)(2,1)S(1)} %collective-permute-done.13), channel_id=1, source_target_pairs={{0,1},{1,2},{2,3},{3,4},{4,5},{5,6},{6,7},{7,8},{8,9},{9,10},{10,1... | collective-permute-start | bytes 1572872 | tf_op jit(solution)/shard_map/ppermute | solution.py:36
  149.4 185.2 %reduce-scatter.2.cloned.1.call-start = ((), (), s32[]{:S(2)}) async-start(), calls=%async_computation.1 | async-start | bytes 8912896 | tf_op jit(solution)/shard_map/reduce_scatter | solution.py:138
  260.8 77.1 %copy-start.2 = (f32[512,256]{1,0:T(8,128)S(1)}, f32[512,256]{1,0:T(8,128)}, u32[]{:S(2)}) copy-start(f32[512,256]{1,0:T(8,128)} %get-tuple-element.35) | copy-start | bytes 1572868
  303.5 0.7 copy-start.4
  334.6 15.1 %collective-permute-start = (bf16[32,8192]{1,0:T(8,128)(2,1)}, bf16[32,8192]{1,0:T(8,128)(2,1)S(1)}, u32[]{:S(2)}, u32[]{:S(2)}) collective-permute-start(bf16[32,8192]{1,0:T(8,128)(2,1)} %reduce-scatter.2.cloned.1.call-done), channel_id=1, source_target_pairs={{16,0},{32,16},{48,32},{64,48},{80,64},{96,80},{112,96},{128,112},... | collective-permute-start | bytes 1572872 | tf_op jit(solution)/shard_map/ppermute | solution.py:55
Sparse Core Ops, SparseCore 0:
  32.4 110.7 all-reduce.4
  149.5 111.2 all-reduce.6
  263.4 71.1 reduce-scatter.1
